TPU v7x, 128 devices: a whole 4x4x4 slice. The times are simulated.
128 devices in a mesh: tm: 32 (over y, z, core), tmpl: 4 (over x).
Axes of the slice: x: 4, y: 4, z: 4, core: 2. Of those that a mesh axis runs over, the one named last changes fastest.
Arguments:
- waveforms: bfloat16 [2000, 131072], P(None, 'tm'), may hold values from -6 to 6
- templates: bfloat16 [64, 96, 512], P('tm', 'tmpl'), may hold values from -6 to 6
- channel_lists: int32 [64, 96], P(None, 'tmpl'), may hold values from 0 to 1999, as said below
- channel_counts: int32 [64], replicated, may hold values from 32 to 96, as said below
- owner_rounds: int32 [4], replicated, may hold values from 0 to 31
Outputs:
- detection: float32 [8, 131072], P(None, ('tm', 'tmpl'))
Inputs may be any that keep to these rules, and one draw needn't show every extreme that they name: `channel_lists`: the 96 channels of one template are distinct. `channel_counts`: slots at or past a template's count are padding; at least one template uses all 96 slots.
All inputs are finite; a program needn't handle non-finite values.
Results may differ from a plain program's by a relative error of at most 0.0003.
Values may be sent and summed in bfloat16 or wider, within the bound.
No kernel may reach another device: no remote copies, remote signals or barrier semaphores. Data moves between devices by JAX's collectives and lax.ppermute only.
A program may use at most 128 MiB of HBM per device.

v0:
```python
import math
import jax
import jax.numpy as jnp
import numpy as np
from jax import lax
from jax.sharding import PartitionSpec as P

stability_floor = 1e-06


def passed_along(array, axis, by):
    size = lax.axis_size(axis)
    pairs = [(i, i + by) for i in range(size) if 0 <= i + by < size]
    return lax.ppermute(array, axis, pairs)


def from_root(array, axis, root):
    mine = lax.axis_index(axis) == root
    return lax.psum(jnp.where(mine, array, jnp.zeros_like(array)), axis)


def shards(waveforms, templates, channel_lists, channel_counts, owner_rounds):
    shard_len = waveforms.shape[1]
    batch_size, slot_dev, tap_count = templates.shape
    stacked = batch_size * slot_dev
    round_count = owner_rounds.shape[0]
    block_len = math.gcd(math.gcd(128, tap_count), shard_len)
    block_count = shard_len // block_len
    tap_blocks = tap_count // block_len
    shift_count = tap_blocks + 1
    kernel_len = shift_count * block_len
    padded_len = tap_count + 2 * block_len
    groups = lax.axis_size("tmpl")
    group_id = lax.axis_index("tmpl")
    slot_ids = group_id * slot_dev + jnp.arange(slot_dev, dtype=jnp.int32)
    lower_triangle_table = jnp.asarray(
        np.arange(block_len)[:, None] < np.arange(block_len)[None, :], jnp.float32
    )
    heads = waveforms[:, :tap_count]
    tail_all = passed_along(heads, "tm", -1)

    def correlate(waveset, picked, tail_rows, usable):
        extended = jnp.concatenate([picked, tail_rows], axis=1)
        blocks = extended.reshape(stacked, block_count + tap_blocks, block_len)
        shifted = jnp.concatenate(
            [blocks[:, shift_id : shift_id + block_count, :] for shift_id in range(shift_count)],
            axis=2,
        )
        waves = waveset.reshape(stacked, tap_count)
        padded = jnp.pad(waves, ((0, 0), (block_len, block_len)))
        tiled = jnp.tile(padded, (1, block_len))[:, block_len:]
        toeplitz = tiled.reshape(stacked, block_len, padded_len - 1)[:, :, :kernel_len]
        correl = jnp.einsum(
            "sbk,sck->sbc", shifted, toeplitz, preferred_element_type=jnp.float32
        ).reshape(stacked, shard_len)
        squared_block_values = jnp.square(blocks.astype(jnp.float32))
        prefix = jnp.einsum(
            "naw,wc->nac",
            squared_block_values,
            lower_triangle_table,
            precision=lax.Precision.HIGHEST,
        )
        totals = jnp.sum(squared_block_values, axis=2)
        window_total = totals[:, 0:block_count]
        for offset in range(1, tap_blocks):
            window_total = window_total + totals[:, offset : offset + block_count]
        energy = (
            window_total[:, :, None]
            - prefix[:, :block_count, :]
            + prefix[:, tap_blocks : tap_blocks + block_count, :]
        )
        energy = energy.reshape(stacked, shard_len)
        wave_f = waves.astype(jnp.float32)
        template_power = jnp.sum(wave_f * wave_f, axis=1)
        normed = correl / (
            jnp.sqrt(jnp.maximum(energy, tap_count / 4.0))
            * jnp.sqrt(template_power + stability_floor)[:, None]
        )
        normed = jnp.where(usable.reshape(stacked, 1), normed, 0.0)
        return jnp.sum(normed.reshape(batch_size, slot_dev, shard_len), axis=1)

    def round_step(round_index, result_rows):
        owner_id = owner_rounds[round_index]
        first_row = owner_id * batch_size
        waveset = from_root(templates, "tm", owner_id)
        chosen = lax.dynamic_slice_in_dim(channel_lists, first_row, batch_size, 0)
        count_rows = lax.dynamic_slice_in_dim(channel_counts, first_row, batch_size, 0)
        chosen_flat = chosen.reshape(stacked)
        picked = jnp.take(waveforms, chosen_flat, axis=0)
        tail_rows = jnp.take(tail_all, chosen_flat, axis=0)
        usable = slot_ids[None, :] < count_rows[:, None]
        local_sum = correlate(waveset, picked, tail_rows, usable)
        share = lax.psum_scatter(local_sum, "tmpl", scatter_dimension=1, tiled=True)
        return lax.dynamic_update_slice_in_dim(result_rows, share, round_index * batch_size, 0)

    result_rows = jnp.zeros((round_count * batch_size, shard_len // groups), jnp.float32)
    return lax.fori_loop(0, round_count, round_step, result_rows)


def solution(mesh):
    in_specs = (P(None, "tm"), P("tm", "tmpl", None), P(None, "tmpl"), P(), P())
    out_specs = P(None, ("tm", "tmpl"))
    return jax.shard_map(shards, mesh=mesh, in_specs=in_specs, out_specs=out_specs, check_vma=False)
```

profile of v0, /device:TPU:1, one launch (start us, length us, event | category | flops | bytes accessed | tf_op | source)
XLA Modules:
  0.0 970.9 jit_solution(954034108740233425)
XLA Ops:
  11.7 24.8 %collective-permute-done = bf16[2000,512]{1,0:T(8,128)(2,1)} collective-permute-done((bf16[2000,512]{1,0:T(8,128)(2,1)S(1)}, bf16[2000,512]{1,0:T(8,128)(2,1)}, u32[]{:S(2)}, u32[]{:S(2)}) %collective-permute-start) | collective-permute-done | bytes 2048032 | tf_op jit(solution)/shard_map/ppermute | solution.py:14
  36.5 927.2 %while.17 = (s32[]{:T(128)}, f32[8,1024]{1,0:T(8,128)S(1)}, s32[4]{0:T(128)S(1)}, s32[64]{0:T(128)S(1)}, s32[64,24]{1,0:T(8,128)S(1)}, /*index=5*/bf16[2000,4096...) while((s32[]{:T(128)}, f32[8,1024]{1,0:T(8,128)S(1)}, ...), condition=%wide.region_6.7_spmd.clone.clone, body=%wide.region_0.6_spmd.sunk.clone.clone.sunk | while | flops 594661696 | bytes 99252792 | solution.py:97
  38.2 8.9 gather_fusion.1
  55.6 119.3 %psum.18 = bf16[2,24,512]{2,1,0:T(8,128)(2,1)S(1)} all-reduce(bf16[2,24,512]{2,1,0:T(8,128)(2,1)S(1)} %broadcast_select_fusion.8), channel_id=1, replica_groups=mesh['tm'=32,'tmpl'=4] {'tm'}, use_global_device_ids=true, to_apply=%region_1.1 | all-reduce | flops 24576 | bytes 98304 | tf_op jit(solution)/shard_map/while/body/eval_jaxpr/psum | solution.py:19
  179.3 12.9 %copy.28 = bf16[6,8,128,768]{3,1,2,0:T(8,128)(2,1)} copy(bf16[6,8,128,768]{3,2,1,0:T(8,128)(2,1)} %bitcast.29) | data formatting | bytes 18874368 | tf_op jit(solution)/shard_map/while
  192.2 7.9 slice.242
  200.1 23.0 %reshape.222 = bf16[48,128,767]{2,1,0:T(8,128)(2,1)} reshape(bf16[48,98176]{1,0:T(8,128)(2,1)} %slice.242) | data formatting | bytes 18849792 | tf_op jit(solution)/shard_map/while/body/eval_jaxpr/reshape | solution.py:52
  223.2 6.6 fusion.26
  234.2 31.0 %reduce-scatter.6.cloned.1.call-done = f32[1024,2]{1,0:T(8,128)} async-done(((f32[4096,2]{1,0:T(8,128)}), f32[1024,2]{1,0:T(8,128)}) %reduce-scatter.6.cloned.1.call-update) | async-done | bytes 8208 | tf_op jit(solution)/shard_map/while
  268.1 8.9 gather_fusion.1
  285.5 123.4 %psum.18 = bf16[2,24,512]{2,1,0:T(8,128)(2,1)S(1)} all-reduce(bf16[2,24,512]{2,1,0:T(8,128)(2,1)S(1)} %broadcast_select_fusion.8), channel_id=1, replica_groups=mesh['tm'=32,'tmpl'=4] {'tm'}, use_global_device_ids=true, to_apply=%region_1.1 | all-reduce | flops 24576 | bytes 98304 | tf_op jit(solution)/shard_map/while/body/eval_jaxpr/psum | solution.py:19
  409.0 4.3 tile.31
  413.3 12.9 %copy.28 = bf16[6,8,128,768]{3,1,2,0:T(8,128)(2,1)} copy(bf16[6,8,128,768]{3,2,1,0:T(8,128)(2,1)} %bitcast.29) | data formatting | bytes 18874368 | tf_op jit(solution)/shard_map/while
  426.2 7.9 slice.242
  434.1 23.0 %reshape.222 = bf16[48,128,767]{2,1,0:T(8,128)(2,1)} reshape(bf16[48,98176]{1,0:T(8,128)(2,1)} %slice.242) | data formatting | bytes 18849792 | tf_op jit(solution)/shard_map/while/body/eval_jaxpr/reshape | solution.py:52
  457.2 6.6 fusion.26
  468.2 29.4 %reduce-scatter.6.cloned.1.call-done = f32[1024,2]{1,0:T(8,128)} async-done(((f32[4096,2]{1,0:T(8,128)}), f32[1024,2]{1,0:T(8,128)}) %reduce-scatter.6.cloned.1.call-update) | async-done | bytes 8208 | tf_op jit(solution)/shard_map/while
  500.5 8.9 gather_fusion.1
  518.0 123.4 %psum.18 = bf16[2,24,512]{2,1,0:T(8,128)(2,1)S(1)} all-reduce(bf16[2,24,512]{2,1,0:T(8,128)(2,1)S(1)} %broadcast_select_fusion.8), channel_id=1, replica_groups=mesh['tm'=32,'tmpl'=4] {'tm'}, use_global_device_ids=true, to_apply=%region_1.1 | all-reduce | flops 24576 | bytes 98304 | tf_op jit(solution)/shard_map/while/body/eval_jaxpr/psum | solution.py:19
  645.7 12.9 %copy.28 = bf16[6,8,128,768]{3,1,2,0:T(8,128)(2,1)} copy(bf16[6,8,128,768]{3,2,1,0:T(8,128)(2,1)} %bitcast.29) | data formatting | bytes 18874368 | tf_op jit(solution)/shard_map/while
  658.7 7.9 slice.242
  666.6 23.0 %reshape.222 = bf16[48,128,767]{2,1,0:T(8,128)(2,1)} reshape(bf16[48,98176]{1,0:T(8,128)(2,1)} %slice.242) | data formatting | bytes 18849792 | tf_op jit(solution)/shard_map/while/body/eval_jaxpr/reshape | solution.py:52
  689.6 6.6 fusion.26
  700.7 29.4 %reduce-scatter.6.cloned.1.call-done = f32[1024,2]{1,0:T(8,128)} async-done(((f32[4096,2]{1,0:T(8,128)}), f32[1024,2]{1,0:T(8,128)}) %reduce-scatter.6.cloned.1.call-update) | async-done | bytes 8208 | tf_op jit(solution)/shard_map/while
  733.0 8.9 gather_fusion.1
  750.4 123.4 %psum.18 = bf16[2,24,512]{2,1,0:T(8,128)(2,1)S(1)} all-reduce(bf16[2,24,512]{2,1,0:T(8,128)(2,1)S(1)} %broadcast_select_fusion.8), channel_id=1, replica_groups=mesh['tm'=32,'tmpl'=4] {'tm'}, use_global_device_ids=true, to_apply=%region_1.1 | all-reduce | flops 24576 | bytes 98304 | tf_op jit(solution)/shard_map/while/body/eval_jaxpr/psum | solution.py:19
  873.9 4.3 tile.31
  878.2 12.9 %copy.28 = bf16[6,8,128,768]{3,1,2,0:T(8,128)(2,1)} copy(bf16[6,8,128,768]{3,2,1,0:T(8,128)(2,1)} %bitcast.29) | data formatting | bytes 18874368 | tf_op jit(solution)/shard_map/while
  891.1 7.9 slice.242
  899.0 23.0 %reshape.222 = bf16[48,128,767]{2,1,0:T(8,128)(2,1)} reshape(bf16[48,98176]{1,0:T(8,128)(2,1)} %slice.242) | data formatting | bytes 18849792 | tf_op jit(solution)/shard_map/while/body/eval_jaxpr/reshape | solution.py:52
  922.1 6.6 fusion.26
  933.1 29.4 %reduce-scatter.6.cloned.1.call-done = f32[1024,2]{1,0:T(8,128)} async-done(((f32[4096,2]{1,0:T(8,128)}), f32[1024,2]{1,0:T(8,128)}) %reduce-scatter.6.cloned.1.call-update) | async-done | bytes 8208 | tf_op jit(solution)/shard_map/while
  (170 shorter events, 71.8 us)
Async XLA Ops:
  6.5 30.0 %copy-start = (f32[128,128,1]{1,0,2:T(8,128)S(1)}, f32[128,128,1]{1,0,2:T(8,128)}, u32[]{:S(2)}) copy-start(f32[128,128,1]{1,0,2:T(8,128)} %constant.217) | copy-start | bytes 196612
  6.5 5.1 copy-start.3
  6.5 30.0 %copy-start.5 = (s32[64]{0:T(128)S(1)}, s32[64]{0:T(128)}, u32[]{:S(2)}) copy-start(s32[64]{0:T(128)} %param.11) | copy-start | bytes 772
  6.5 30.0 %copy-start.4 = (s32[4]{0:T(128)S(1)}, s32[4]{0:T(128)}, u32[]{:S(2)}) copy-start(s32[4]{0:T(128)} %param.12) | copy-start | bytes 52
  6.5 30.0 %copy-start.1 = (bf16[2,24,512]{2,1,0:T(8,128)(2,1)S(1)}, bf16[2,24,512]{2,1,0:T(8,128)(2,1)}, u32[]{:S(2)}) copy-start(bf16[2,24,512]{2,1,0:T(8,128)(2,1)} %param.9) | copy-start | bytes 147460
  8.3 28.2 %collective-permute-start = (bf16[2000,512]{1,0:T(8,128)(2,1)S(1)}, bf16[2000,512]{1,0:T(8,128)(2,1)}, u32[]{:S(2)}, u32[]{:S(2)}) collective-permute-start(bf16[2000,512]{1,0:T(8,128)(2,1)S(1)} %slice.133), channel_id=1, source_target_pairs={{4,0},{8,4},{12,8},{16,12},{20,16},{24,20},{28,24},{32,28},{36,32}... | collective-permute-start | bytes 6144008 | tf_op jit(solution)/shard_map/ppermute | solution.py:14
  36.6 228.7 %reduce-scatter.6.cloned.1.call-start = ((), (), s32[]{:S(2)}) async-start(), calls=%async_computation.1 | async-start | bytes 2621440 | tf_op jit(solution)/shard_map/while
  266.5 231.2 %reduce-scatter.6.cloned.1.call-start = ((), (), s32[]{:S(2)}) async-start(), calls=%async_computation.1 | async-start | bytes 2621440 | tf_op jit(solution)/shard_map/while
  498.9 231.2 %reduce-scatter.6.cloned.1.call-start = ((), (), s32[]{:S(2)}) async-start(), calls=%async_computation.1 | async-start | bytes 2621440 | tf_op jit(solution)/shard_map/while
  731.4 231.2 %reduce-scatter.6.cloned.1.call-start = ((), (), s32[]{:S(2)}) async-start(), calls=%async_computation.1 | async-start | bytes 2621440 | tf_op jit(solution)/shard_map/while
  963.8 0.6 copy-start.2
Sparse Core Ops, SparseCore 0:
  234.3 30.8 reduce-scatter.5
  468.3 29.2 reduce-scatter.5
  700.8 29.2 reduce-scatter.5
  933.2 29.2 reduce-scatter.5
where the time goes:
time: 972 us; the launch traced here: 971 us
  blocking collectives  489 us (50%)
  local copies, waits for them, and re-layouts  279 us (29%)
  waiting for transfers between devices  144 us (15%)
  matrix products  29.9 us (3%)
  between operations  13.1 us (1%)
    psum x4, blocking collectives, from_root(): return lax.psum(jnp.where(mine, array, jnp.zeros_like(array)), axis)  489 us
    while x8, waiting for transfers between devices  119 us
    reshape x4, local copies, waits for them, and re-layouts, correlate(): tiled.reshape(stacked, block_len, padded_len - 1)[:, :, :kernel_len]  92.1 us
    while x28, local copies, waits for them, and re-layouts  78.9 us
    gather x4, local copies, waits for them, and re-layouts, round_step(): picked = jnp.take(waveforms, chosen_flat, axis=0)  35.7 us
    slice x4, local copies, waits for them, and re-layouts, correlate(): tiled = jnp.tile(padded, (1, block_len))[:, block_len:]  31.7 us
    dot_general x4, matrix products, correlate(): jnp.einsum('sbk,sck->sbc', shifted, toeplitz, preferred_element_type=jnp....  26.4 us
    ppermute x1, waiting for transfers between devices, passed_along(): return lax.ppermute(array, axis, pairs)  24.8 us
  transfers between devices with their start and end apart: 5, of which 5 were waited for; matrix products, arithmetic and copies ran while one was open for 0% of the time, Pallas kernels for 0%

commit v1 on v0

--- a/solution.py
+++ b/solution.py
@@ -16,7 +16,7 @@
 
 def from_root(array, axis, root):
     mine = lax.axis_index(axis) == root
-    return lax.psum(jnp.where(mine, array, jnp.zeros_like(array)), axis)
+    return jnp.sum(lax.all_gather(jnp.where(mine, array, jnp.zeros_like(array)), axis), axis=0)
 
 
 def shards(waveforms, templates, channel_lists, channel_counts, owner_rounds):

time: 972 us -> 590 us (0.61)
  blocking collectives: 489 us -> 0 us
  waiting for transfers between devices: 144 us -> 243 us
    psum x4 -> x0, blocking collectives: 489 us -> none  [from_root(): return lax.psum(jnp.where(mine, array, jnp.zeros_like(array)), axis)]
    all_gather x0 -> x4, waiting for transfers between devices: none -> 104 us  [from_root(): lax.all_gather(jnp.where(mine, array, jnp.zeros_like(array)), axis)]
    while x8 -> x12, waiting for transfers between devices: 119 us -> 114 us
  transfers between devices with their start and end apart: 5 -> 9, of which waited for: 5 -> 9; matrix products, arithmetic and copies ran while one was open for 0% -> 13% of each run, Pallas kernels for 0% -> 0%
where the time goes in v1:
time: 590 us; the launch traced here: 588 us
  local copies, waits for them, and re-layouts  279 us (47%)
  waiting for transfers between devices  243 us (41%)
  matrix products  29.9 us (5%)
  other arithmetic  14.7 us (2%)
  between operations  13.4 us (2%)
    while x12, waiting for transfers between devices  114 us
    all_gather x4, waiting for transfers between devices, from_root(): lax.all_gather(jnp.where(mine, array, jnp.zeros_like(array)), axis)  104 us
    reshape x4, local copies, waits for them, and re-layouts, correlate(): tiled.reshape(stacked, block_len, padded_len - 1)[:, :, :kernel_len]  92.1 us
    while x28, local copies, waits for them, and re-layouts  78.9 us
    gather x4, local copies, waits for them, and re-layouts, round_step(): picked = jnp.take(waveforms, chosen_flat, axis=0)  35.7 us
    slice x4, local copies, waits for them, and re-layouts, correlate(): tiled = jnp.tile(padded, (1, block_len))[:, block_len:]  31.7 us
    dot_general x4, matrix products, correlate(): jnp.einsum('sbk,sck->sbc', shifted, toeplitz, preferred_element_type=jnp....  26.4 us
    ppermute x1, waiting for transfers between devices, passed_along(): return lax.ppermute(array, axis, pairs)  24.8 us
  transfers between devices with their start and end apart: 9, of which 9 were waited for; matrix products, arithmetic and copies ran while one was open for 13% of the time, Pallas kernels for 0%

profile of v1, /device:TPU:1, one launch (start us, length us, event | category | flops | bytes accessed | tf_op | source)
XLA Modules:
  0.0 588.4 jit_solution(13650563951188559738)
XLA Ops:
  11.7 24.8 %collective-permute-done = bf16[2000,512]{1,0:T(8,128)(2,1)} collective-permute-done((bf16[2000,512]{1,0:T(8,128)(2,1)S(1)}, bf16[2000,512]{1,0:T(8,128)(2,1)}, u32[]{:S(2)}, u32[]{:S(2)}) %collective-permute-start) | collective-permute-done | bytes 2048032 | tf_op jit(solution)/shard_map/ppermute | solution.py:14
  36.5 544.4 %while.18 = (s32[]{:T(128)}, f32[8,1024]{1,0:T(8,128)S(1)}, s32[4]{0:T(128)S(1)}, s32[64]{0:T(128)S(1)}, s32[64,24]{1,0:T(8,128)S(1)}, /*index=5*/bf16[2000,4096...) while((s32[]{:T(128)}, f32[8,1024]{1,0:T(8,128)S(1)}, ...), condition=%wide.region_6.7_spmd.clone.clone, body=%wide.region_0.6_spmd.sunk.clone.clone.sunk | while | flops 595398976 | bytes 105642584 | solution.py:97
  39.3 8.9 %gather_fusion.1 = bf16[48,4096]{1,0:T(8,128)(2,1)S(1)} fusion(bf16[2000,4096]{1,0:T(8,128)(2,1)} %get-tuple-element.472, s32[1024]{0:T(1024)S(1)} %pad_clamp_fusion.2), kind=kCustom, calls=%fused_computation.clone.clone.1 | custom fusion | bytes 786624 | tf_op jit(solution)/shard_map/while/body/eval_jaxpr/jit(_take)/gather | solution.py:89
  57.9 28.7 %all-gather.6.cloned.1.call-done = bf16[64,24,512]{2,1,0:T(8,128)(2,1)} async-done(((bf16[2,24,512]{2,1,0:T(8,128)(2,1)}), bf16[64,24,512]{2,1,0:T(8,128)(2,1)}) %all-gather.6.cloned.1.call-update) | async-done | bytes 1572880 | tf_op jit(solution)/shard_map/while/body/eval_jaxpr/all_gather | solution.py:19
  92.7 12.9 %copy.28 = bf16[6,8,128,768]{3,1,2,0:T(8,128)(2,1)} copy(bf16[6,8,128,768]{3,2,1,0:T(8,128)(2,1)} %bitcast.32) | data formatting | bytes 18874368 | tf_op jit(solution)/shard_map/while
  105.6 7.9 %slice.255 = bf16[48,98176]{1,0:T(8,128)(2,1)} slice(bf16[48,98304]{1,0:T(8,128)(2,1)} %bitcast.33), slice={[0:48], [128:98304]} | slice | bytes 18849792 | tf_op jit(solution)/shard_map/while/body/eval_jaxpr/slice | solution.py:51
  113.6 23.0 %reshape.249 = bf16[48,128,767]{2,1,0:T(8,128)(2,1)} reshape(bf16[48,98176]{1,0:T(8,128)(2,1)} %slice.255) | data formatting | bytes 18849792 | tf_op jit(solution)/shard_map/while/body/eval_jaxpr/reshape | solution.py:52
  136.6 6.6 %fusion.26 = f32[48,32,128]{2,1,0:T(8,128)S(1)} fusion(bf16[48,32,640]{2,1,0:T(8,128)(2,1)} %slice_dynamic-update-slice_fusion.14, bf16[48,128,767]{2,1,0:T(8,128)(2,1)} %reshape.249), kind=kOutput, calls=%fused_computation.3.clone.1 | convolution fusion | flops 251658240 | bytes 10616832 | tf_op jit(solution)/shard_map/while/body/eval_jaxpr/sbk,sck->sbc/dot_general | solution.py:53
  145.7 28.5 %reduce-scatter.6.cloned.1.call-done = f32[1024,2]{1,0:T(8,128)} async-done(((f32[4096,2]{1,0:T(8,128)}), f32[1024,2]{1,0:T(8,128)}) %reduce-scatter.6.cloned.1.call-update) | async-done | bytes 8208 | tf_op jit(solution)/shard_map/while
  178.2 8.9 %gather_fusion.1 = bf16[48,4096]{1,0:T(8,128)(2,1)S(1)} fusion(bf16[2000,4096]{1,0:T(8,128)(2,1)} %get-tuple-element.472, s32[1024]{0:T(1024)S(1)} %pad_clamp_fusion.2), kind=kCustom, calls=%fused_computation.clone.clone.1 | custom fusion | bytes 786624 | tf_op jit(solution)/shard_map/while/body/eval_jaxpr/jit(_take)/gather | solution.py:89
  196.9 25.0 %all-gather.6.cloned.1.call-done = bf16[64,24,512]{2,1,0:T(8,128)(2,1)} async-done(((bf16[2,24,512]{2,1,0:T(8,128)(2,1)}), bf16[64,24,512]{2,1,0:T(8,128)(2,1)}) %all-gather.6.cloned.1.call-update) | async-done | bytes 1572880 | tf_op jit(solution)/shard_map/while/body/eval_jaxpr/all_gather | solution.py:19
  227.9 12.9 %copy.28 = bf16[6,8,128,768]{3,1,2,0:T(8,128)(2,1)} copy(bf16[6,8,128,768]{3,2,1,0:T(8,128)(2,1)} %bitcast.32) | data formatting | bytes 18874368 | tf_op jit(solution)/shard_map/while
  240.8 7.9 %slice.255 = bf16[48,98176]{1,0:T(8,128)(2,1)} slice(bf16[48,98304]{1,0:T(8,128)(2,1)} %bitcast.33), slice={[0:48], [128:98304]} | slice | bytes 18849792 | tf_op jit(solution)/shard_map/while/body/eval_jaxpr/slice | solution.py:51
  248.8 23.0 %reshape.249 = bf16[48,128,767]{2,1,0:T(8,128)(2,1)} reshape(bf16[48,98176]{1,0:T(8,128)(2,1)} %slice.255) | data formatting | bytes 18849792 | tf_op jit(solution)/shard_map/while/body/eval_jaxpr/reshape | solution.py:52
  271.8 6.6 %fusion.26 = f32[48,32,128]{2,1,0:T(8,128)S(1)} fusion(bf16[48,32,640]{2,1,0:T(8,128)(2,1)} %slice_dynamic-update-slice_fusion.14, bf16[48,128,767]{2,1,0:T(8,128)(2,1)} %reshape.249), kind=kOutput, calls=%fused_computation.3.clone.1 | convolution fusion | flops 251658240 | bytes 10616832 | tf_op jit(solution)/shard_map/while/body/eval_jaxpr/sbk,sck->sbc/dot_general | solution.py:53
  280.9 28.5 %reduce-scatter.6.cloned.1.call-done = f32[1024,2]{1,0:T(8,128)} async-done(((f32[4096,2]{1,0:T(8,128)}), f32[1024,2]{1,0:T(8,128)}) %reduce-scatter.6.cloned.1.call-update) | async-done | bytes 8208 | tf_op jit(solution)/shard_map/while
  313.4 8.9 %gather_fusion.1 = bf16[48,4096]{1,0:T(8,128)(2,1)S(1)} fusion(bf16[2000,4096]{1,0:T(8,128)(2,1)} %get-tuple-element.472, s32[1024]{0:T(1024)S(1)} %pad_clamp_fusion.2), kind=kCustom, calls=%fused_computation.clone.clone.1 | custom fusion | bytes 786624 | tf_op jit(solution)/shard_map/while/body/eval_jaxpr/jit(_take)/gather | solution.py:89
  332.1 24.8 %all-gather.6.cloned.1.call-done = bf16[64,24,512]{2,1,0:T(8,128)(2,1)} async-done(((bf16[2,24,512]{2,1,0:T(8,128)(2,1)}), bf16[64,24,512]{2,1,0:T(8,128)(2,1)}) %all-gather.6.cloned.1.call-update) | async-done | bytes 1572880 | tf_op jit(solution)/shard_map/while/body/eval_jaxpr/all_gather | solution.py:19
  358.6 4.3 tile.32
  362.9 12.9 %copy.28 = bf16[6,8,128,768]{3,1,2,0:T(8,128)(2,1)} copy(bf16[6,8,128,768]{3,2,1,0:T(8,128)(2,1)} %bitcast.32) | data formatting | bytes 18874368 | tf_op jit(solution)/shard_map/while
  375.8 7.9 %slice.255 = bf16[48,98176]{1,0:T(8,128)(2,1)} slice(bf16[48,98304]{1,0:T(8,128)(2,1)} %bitcast.33), slice={[0:48], [128:98304]} | slice | bytes 18849792 | tf_op jit(solution)/shard_map/while/body/eval_jaxpr/slice | solution.py:51
  383.8 23.0 %reshape.249 = bf16[48,128,767]{2,1,0:T(8,128)(2,1)} reshape(bf16[48,98176]{1,0:T(8,128)(2,1)} %slice.255) | data formatting | bytes 18849792 | tf_op jit(solution)/shard_map/while/body/eval_jaxpr/reshape | solution.py:52
  406.8 6.6 %fusion.26 = f32[48,32,128]{2,1,0:T(8,128)S(1)} fusion(bf16[48,32,640]{2,1,0:T(8,128)(2,1)} %slice_dynamic-update-slice_fusion.14, bf16[48,128,767]{2,1,0:T(8,128)(2,1)} %reshape.249), kind=kOutput, calls=%fused_computation.3.clone.1 | convolution fusion | flops 251658240 | bytes 10616832 | tf_op jit(solution)/shard_map/while/body/eval_jaxpr/sbk,sck->sbc/dot_general | solution.py:53
  415.9 28.5 %reduce-scatter.6.cloned.1.call-done = f32[1024,2]{1,0:T(8,128)} async-done(((f32[4096,2]{1,0:T(8,128)}), f32[1024,2]{1,0:T(8,128)}) %reduce-scatter.6.cloned.1.call-update) | async-done | bytes 8208 | tf_op jit(solution)/shard_map/while
  448.4 8.9 %gather_fusion.1 = bf16[48,4096]{1,0:T(8,128)(2,1)S(1)} fusion(bf16[2000,4096]{1,0:T(8,128)(2,1)} %get-tuple-element.472, s32[1024]{0:T(1024)S(1)} %pad_clamp_fusion.2), kind=kCustom, calls=%fused_computation.clone.clone.1 | custom fusion | bytes 786624 | tf_op jit(solution)/shard_map/while/body/eval_jaxpr/jit(_take)/gather | solution.py:89
  467.1 25.0 %all-gather.6.cloned.1.call-done = bf16[64,24,512]{2,1,0:T(8,128)(2,1)} async-done(((bf16[2,24,512]{2,1,0:T(8,128)(2,1)}), bf16[64,24,512]{2,1,0:T(8,128)(2,1)}) %all-gather.6.cloned.1.call-update) | async-done | bytes 1572880 | tf_op jit(solution)/shard_map/while/body/eval_jaxpr/all_gather | solution.py:19
  493.9 4.3 tile.32
  498.1 12.9 %copy.28 = bf16[6,8,128,768]{3,1,2,0:T(8,128)(2,1)} copy(bf16[6,8,128,768]{3,2,1,0:T(8,128)(2,1)} %bitcast.32) | data formatting | bytes 18874368 | tf_op jit(solution)/shard_map/while
  511.1 7.9 %slice.255 = bf16[48,98176]{1,0:T(8,128)(2,1)} slice(bf16[48,98304]{1,0:T(8,128)(2,1)} %bitcast.33), slice={[0:48], [128:98304]} | slice | bytes 18849792 | tf_op jit(solution)/shard_map/while/body/eval_jaxpr/slice | solution.py:51
  519.0 23.0 %reshape.249 = bf16[48,128,767]{2,1,0:T(8,128)(2,1)} reshape(bf16[48,98176]{1,0:T(8,128)(2,1)} %slice.255) | data formatting | bytes 18849792 | tf_op jit(solution)/shard_map/while/body/eval_jaxpr/reshape | solution.py:52
  542.0 6.6 %fusion.26 = f32[48,32,128]{2,1,0:T(8,128)S(1)} fusion(bf16[48,32,640]{2,1,0:T(8,128)(2,1)} %slice_dynamic-update-slice_fusion.14, bf16[48,128,767]{2,1,0:T(8,128)(2,1)} %reshape.249), kind=kOutput, calls=%fused_computation.3.clone.1 | convolution fusion | flops 251658240 | bytes 10616832 | tf_op jit(solution)/shard_map/while/body/eval_jaxpr/sbk,sck->sbc/dot_general | solution.py:53
  551.1 28.5 %reduce-scatter.6.cloned.1.call-done = f32[1024,2]{1,0:T(8,128)} async-done(((f32[4096,2]{1,0:T(8,128)}), f32[1024,2]{1,0:T(8,128)}) %reduce-scatter.6.cloned.1.call-update) | async-done | bytes 8208 | tf_op jit(solution)/shard_map/while
  (182 shorter events, 80.9 us)
Async XLA Ops:
  6.5 30.0 %copy-start = (f32[128,128,1]{1,0,2:T(8,128)S(1)}, f32[128,128,1]{1,0,2:T(8,128)}, u32[]{:S(2)}) copy-start(f32[128,128,1]{1,0,2:T(8,128)} %constant.234) | copy-start | bytes 196612
  6.5 5.1 copy-start.3
  6.5 30.0 %copy-start.5 = (s32[64]{0:T(128)S(1)}, s32[64]{0:T(128)}, u32[]{:S(2)}) copy-start(s32[64]{0:T(128)} %param.11) | copy-start | bytes 772
  6.5 30.0 %copy-start.4 = (s32[4]{0:T(128)S(1)}, s32[4]{0:T(128)}, u32[]{:S(2)}) copy-start(s32[4]{0:T(128)} %param.12) | copy-start | bytes 52
  6.5 30.0 %copy-start.1 = (bf16[2,24,512]{2,1,0:T(8,128)(2,1)S(1)}, bf16[2,24,512]{2,1,0:T(8,128)(2,1)}, u32[]{:S(2)}) copy-start(bf16[2,24,512]{2,1,0:T(8,128)(2,1)} %param.9) | copy-start | bytes 147460
  8.3 28.2 %collective-permute-start = (bf16[2000,512]{1,0:T(8,128)(2,1)S(1)}, bf16[2000,512]{1,0:T(8,128)(2,1)}, u32[]{:S(2)}, u32[]{:S(2)}) collective-permute-start(bf16[2000,512]{1,0:T(8,128)(2,1)S(1)} %slice.146), channel_id=1, source_target_pairs={{4,0},{8,4},{12,8},{16,12},{20,16},{24,20},{28,24},{32,28},{36,32}... | collective-permute-start | bytes 6144008 | tf_op jit(solution)/shard_map/ppermute | solution.py:14
  36.6 50.1 %all-gather.6.cloned.1.call-start = ((), (), s32[]{:S(2)}) async-start(), calls=%async_computation.1 | async-start | bytes 1622016 | tf_op jit(solution)/shard_map/while/body/eval_jaxpr/all_gather | solution.py:19
  38.4 135.8 %reduce-scatter.6.cloned.1.call-start = ((), (), s32[]{:S(2)}) async-start(), calls=%async_computation.2 | async-start | bytes 2621440 | tf_op jit(solution)/shard_map/while
  175.5 46.4 %all-gather.6.cloned.1.call-start = ((), (), s32[]{:S(2)}) async-start(), calls=%async_computation.1 | async-start | bytes 1622016 | tf_op jit(solution)/shard_map/while/body/eval_jaxpr/all_gather | solution.py:19
  177.4 132.1 %reduce-scatter.6.cloned.1.call-start = ((), (), s32[]{:S(2)}) async-start(), calls=%async_computation.2 | async-start | bytes 2621440 | tf_op jit(solution)/shard_map/while
  310.7 46.2 %all-gather.6.cloned.1.call-start = ((), (), s32[]{:S(2)}) async-start(), calls=%async_computation.1 | async-start | bytes 1622016 | tf_op jit(solution)/shard_map/while/body/eval_jaxpr/all_gather | solution.py:19
  312.6 131.9 %reduce-scatter.6.cloned.1.call-start = ((), (), s32[]{:S(2)}) async-start(), calls=%async_computation.2 | async-start | bytes 2621440 | tf_op jit(solution)/shard_map/while
  445.7 46.4 %all-gather.6.cloned.1.call-start = ((), (), s32[]{:S(2)}) async-start(), calls=%async_computation.1 | async-start | bytes 1622016 | tf_op jit(solution)/shard_map/while/body/eval_jaxpr/all_gather | solution.py:19
  447.6 132.1 %reduce-scatter.6.cloned.1.call-start = ((), (), s32[]{:S(2)}) async-start(), calls=%async_computation.2 | async-start | bytes 2621440 | tf_op jit(solution)/shard_map/while
  580.9 0.6 copy-start.2
Sparse Core Ops, SparseCore 0:
  39.6 47.0 all-gather.5
  145.8 28.3 reduce-scatter.5
  178.6 43.3 all-gather.5
  281.0 28.3 reduce-scatter.5
  313.5 43.3 all-gather.5
  416.0 28.3 reduce-scatter.5
  448.8 43.3 all-gather.5
  551.3 28.3 reduce-scatter.5
